TPU v7x, 32 devices: a whole 2x2x4 slice. The times are simulated.
32 devices in a mesh: hi: 4 (over z), mid: 4 (over x, core), lo: 2 (over y).
Axes of the slice: x: 2, y: 2, z: 4, core: 2. Of those that a mesh axis runs over, the one named last changes fastest.
Arguments:
- amplitudes: bfloat16 [1024, 16384], P('lo', ('hi', 'mid')), may hold values from -6 to 6
- hop_blocks: bfloat16 [4, 512, 512], replicated, may hold values from -1 to 2, as said below
- coupling_seed: int32 [14], replicated, may hold values from 1 to 7
Outputs:
- new_state: bfloat16 [1024, 16384], P('lo', ('hi', 'mid'))
Inputs may be any that keep to these rules, and one draw needn't show every extreme that they name: hop_blocks[k, a, b] is zero where a and b differ in their number of set bits.
All inputs are finite; a program needn't handle non-finite values.
Results may differ from a plain program's by a relative error of at most 0.0064.
Values may be sent and summed in bfloat16 or wider, within the bound.
A program may use at most 64 MiB of HBM per device.

v0:
```python
import jax
import jax.numpy as jnp
from jax import lax
from jax.sharding import PartitionSpec as P

BLOCK = 512
SITES = 14


COUPLING = 0.06


def occupancy(indices):
    site_ids = jnp.arange(SITES, dtype=jnp.int32)
    return (indices[:, None] >> site_ids[None, :] & 1).astype(jnp.float32)


def diagonal_factor(up_index, down_index, coupling_seed):
    up_occupied = occupancy(up_index)
    down_occupied = occupancy(down_index)
    strength = COUPLING * coupling_seed.astype(jnp.float32)
    energy = jnp.dot(
        up_occupied * strength[None, :], down_occupied.T, precision=lax.Precision.HIGHEST
    )
    return jnp.exp(-energy)


def on_device(amplitudes, hop_blocks, coupling_seed):
    down_rows, up_cols = amplitudes.shape
    groups = lax.axis_size(("hi", "mid"))
    lo_count = lax.axis_size("lo")
    split_view = amplitudes.reshape(down_rows, up_cols // BLOCK, BLOCK)
    first_pass = jnp.einsum(
        "dav,wv->awd", split_view, hop_blocks[0], preferred_element_type=jnp.float32
    ).astype(jnp.bfloat16)
    local_top = BLOCK // groups
    remainder = up_cols // local_top
    first_pass = first_pass.reshape(local_top, remainder, down_rows)
    moved = lax.all_to_all(first_pass, ("hi", "mid"), split_axis=1, concat_axis=0, tiled=True)
    second_pass = jnp.einsum(
        "gh,hpd->gpd", hop_blocks[1], moved, preferred_element_type=jnp.float32
    )
    span_low = remainder // groups
    up_index = (
        jnp.arange(BLOCK, dtype=jnp.int32)[:, None] * remainder
        + lax.axis_index(("hi", "mid")) * span_low
        + jnp.arange(span_low, dtype=jnp.int32)[None, :]
    ).reshape(-1)
    down_index = lax.axis_index("lo") * down_rows + jnp.arange(down_rows, dtype=jnp.int32)
    factor = diagonal_factor(up_index, down_index, coupling_seed).reshape(
        BLOCK, span_low, down_rows
    )
    mixed_pass = (second_pass * factor).astype(jnp.bfloat16)
    returned = lax.all_to_all(
        mixed_pass, ("hi", "mid"), split_axis=0, concat_axis=1, tiled=True
    ).reshape(up_cols, down_rows)
    third_pass = jnp.einsum(
        "ud,ed->eu", returned, hop_blocks[2], preferred_element_type=jnp.float32
    ).astype(jnp.bfloat16)
    gathered = lax.all_to_all(
        third_pass.reshape(BLOCK // lo_count, lo_count, up_cols),
        "lo",
        split_axis=1,
        concat_axis=0,
        tiled=True,
    )
    fourth_pass = jnp.einsum(
        "gh,hpu->gpu", hop_blocks[3], gathered, preferred_element_type=jnp.float32
    ).astype(jnp.bfloat16)
    result = lax.all_to_all(fourth_pass, "lo", split_axis=0, concat_axis=1, tiled=True).reshape(
        down_rows, up_cols
    )
    return result


def solution(mesh):
    in_specs = (P("lo", ("hi", "mid")), P(), P())
    out_specs = P("lo", ("hi", "mid"))
    return jax.shard_map(
        on_device, mesh=mesh, in_specs=in_specs, out_specs=out_specs, check_vma=False
    )
```

profile of v0, /device:TPU:0, one launch (start us, length us, event | category | flops | bytes accessed | tf_op | source)
XLA Modules:
  0.0 115.0 jit_solution(5764832066527705775)
XLA Ops:
  0.0 2.1 %convolution_convert_fusion.2 = bf16[512,512,2]{1,0,2:T(8,128)(2,1)S(1)} fusion(bf16[64,2,8,512]{3,2,1,0:T(8,128)(2,1)} %bitcast.57, bf16[4,512,512]{2,1,0:T(8,128)(2,1)} %param.4), kind=kOutput, calls=%fused_computation.5 | convolution fusion | flops 537395200 | bytes 2621440 | tf_op jit(solution)/shard_map/dav,wv->awd/dot_general | solution.py:33
  2.1 1.5 %copy.56 = bf16[32,32,512]{2,0,1:T(8,128)(2,1)} copy(bf16[32,32,512]{2,1,0:T(8,128)(2,1)S(1)} %bitcast.56) | data formatting | bytes 2097152 | tf_op jit(solution)/shard_map/reshape | solution.py:38
  3.7 7.4 %all-to-all-start = ((bf16[32,32,512]{2,0,1:T(8,128)(2,1)}), bf16[32,32,512]{2,0,1:T(8,128)(2,1)S(1)}, u32[]{:S(2)}, u32[]{:S(2)}) async-start(bf16[32,32,512]{2,0,1:T(8,128)(2,1)} %copy.56), calls=%async_computation | async-start | bytes 2097152 | tf_op jit(solution)/shard_map/all_to_all | solution.py:39
  11.5 2.0 %negate_exponential_fusion = f32[1024,512]{1,0:T(8,128)S(1)} fusion(s32[512]{0:T(512)S(1)} %iota_add_fusion.1, f32[14]{0:T(128)S(1)} %convert_multiply_fusion, s32[1024]{0:T(1024)S(1)} %add.50), kind=kOutput, calls=%fused_computation.2 | convolution fusion | flops 88683520 | bytes 2103352 | tf_op jit(solution)/shard_map/dot_general | solution.py:22
  13.4 2.3 %reshape.54 = f32[512,2,512]{2,1,0:T(2,128)} reshape(f32[1024,512]{1,0:T(8,128)S(1)} %negate_exponential_fusion) | data formatting | bytes 4194304 | tf_op jit(solution)/shard_map/reshape | solution.py:50
  15.7 2.7 %copy.59 = f32[512,2,512]{0,2,1:T(8,128)S(1)} copy(f32[512,2,512]{2,1,0:T(2,128)} %reshape.54) | data formatting | bytes 4194304 | tf_op jit(solution)/shard_map/reshape | solution.py:50
  18.5 15.5 %all-to-all-done = bf16[32,32,512]{2,0,1:T(8,128)(2,1)S(1)} async-done(((bf16[32,32,512]{2,0,1:T(8,128)(2,1)}), bf16[32,32,512]{2,0,1:T(8,128)(2,1)S(1)}, u32[]{:S(2)}, u32[]{:S(2)}) %all-to-all-start) | async-done | bytes 1048608 | tf_op jit(solution)/shard_map/all_to_all | solution.py:39
  34.1 1.8 %fusion = bf16[512,2,512]{0,2,1:T(8,128)(2,1)S(1)} fusion(f32[512,2,512]{0,2,1:T(8,128)S(1)} %copy.59, bf16[512,2,512]{2,0,1:T(8,128)(2,1)S(1)} %bitcast.54, bf16[4,512,512]{2,1,0:T(8,128)(2,1)} %param.4), kind=kOutput, calls=%fused_computation.1 | convolution fusion | flops 537919488 | bytes 4718592 | tf_op jit(solution)/shard_map/gh,hpd->gpd/dot_general | solution.py:40
  35.9 1.0 copy.60
  36.9 31.3 %all_to_all.63 = bf16[512,2,512]{2,1,0:T(2,128)(2,1)S(1)} all-to-all(bf16[512,2,512]{2,1,0:T(2,128)(2,1)S(1)} %copy.60), channel_id=1, replica_groups=mesh['hi'=4,'mid'=4,'lo'=2] {'hi','mid'}, dimensions={0} | all-to-all | bytes 2097152 | tf_op jit(solution)/shard_map/all_to_all | solution.py:54
  68.3 1.1 copy.62
  69.4 0.4 reshape.55
  69.8 1.8 %fusion.1 = bf16[512,1024]{1,0:T(8,128)(2,1)S(1)} fusion(bf16[1024,512]{1,0:T(8,128)(2,1)S(1)} %reshape.55, bf16[4,512,512]{2,1,0:T(8,128)(2,1)} %param.4), kind=kOutput, calls=%fused_computation.6 | convolution fusion | flops 537395200 | bytes 2621440 | tf_op jit(solution)/shard_map/ud,ed->eu/dot_general | solution.py:57
  71.6 0.4 reshape.56
  72.4 17.5 %all_to_all.64 = bf16[256,2,1024]{2,0,1:T(8,128)(2,1)S(1)} all-to-all(bf16[256,2,1024]{2,0,1:T(8,128)(2,1)S(1)} %copy.63), channel_id=1, replica_groups=mesh['hi'=4,'mid'=4,'lo'=2] {'lo'}, dimensions={1} | all-to-all | bytes 2097152 | tf_op jit(solution)/shard_map/all_to_all | solution.py:60
  89.8 1.8 %fusion.2 = bf16[512,1,1024]{0,2,1:T(8,128)(2,1)S(1)} fusion(bf16[512,1024]{1,0:T(8,128)(2,1)S(1)} %bitcast.55, bf16[4,512,512]{2,1,0:T(8,128)(2,1)} %param.4), kind=kOutput, calls=%fused_computation.7 | convolution fusion | flops 537395200 | bytes 2621440 | tf_op jit(solution)/shard_map/gh,hpu->gpu/dot_general | solution.py:67
  91.6 0.5 broadcast.24
  92.1 1.5 %reduce = bf16[512,1024]{0,1:T(8,128)(2,1)S(1)} reduce(bf16[512,1,1024]{0,2,1:T(8,128)(2,1)S(1)} %fusion.2, bf16[]{:T(256)} %broadcast.24), dimensions={1}, to_apply=%copy.64.reduce_sub_computation | reduce | bytes 2097154 | tf_op jit(solution)/shard_map/convert_element_type | solution.py:69
  93.6 0.5 copy.73
  94.1 0.8 reshape.61
  94.9 16.5 %all_to_all.65 = bf16[2,2,131072]{2,1,0:T(2,128)(2,1)S(1)} all-to-all(bf16[2,2,131072]{2,1,0:T(2,128)(2,1)S(1)} %reshape.61), channel_id=1, replica_groups=mesh['hi'=4,'mid'=4,'lo'=2] {'lo'}, dimensions={0} | all-to-all | bytes 2097152 | tf_op jit(solution)/shard_map/all_to_all | solution.py:70
  111.4 0.9 reshape.62
  112.7 1.1 copy.65
  113.8 1.2 %reshape.58 = bf16[512,1024]{1,0:T(8,128)(2,1)} reshape(bf16[256,2,1,1024]{3,1,0,2:T(2,128)(2,1)S(1)} %copy.65) | data formatting | bytes 2097152 | tf_op jit(solution)/shard_map/reshape | solution.py:70
  (11 shorter events, 1.2 us)
Async XLA Ops:
  2.1 9.3 %copy-start = (s32[14]{0:T(128)S(1)}, s32[14]{0:T(128)}, u32[]{:S(2)}) copy-start(s32[14]{0:T(128)} %param.5) | copy-start | bytes 172
  3.7 30.3 %all-to-all-start = ((bf16[32,32,512]{2,0,1:T(8,128)(2,1)}), bf16[32,32,512]{2,0,1:T(8,128)(2,1)S(1)}, u32[]{:S(2)}, u32[]{:S(2)}) async-start(bf16[32,32,512]{2,0,1:T(8,128)(2,1)} %copy.56), calls=%async_computation | async-start | bytes 2097152 | tf_op jit(solution)/shard_map/all_to_all | solution.py:39
where the time goes:
time: 116 us; the launch traced here: 115 us
  blocking collectives  65.2 us (56%)
  local copies, waits for them, and re-layouts  15.7 us (14%)
  waiting for transfers between devices  15.5 us (13%)
  matrix products  9.51 us (8%)
  starting transfers between devices  7.39 us (6%)
  other arithmetic  1.59 us (1%)
    all_to_all x1, blocking collectives, on_device(): lax.all_to_all(mixed_pass, ('hi', 'mid'), split_axis=0, concat_axis=1, ti...  31.3 us
    all_to_all x1, blocking collectives, on_device(): lax.all_to_all(third_pass.reshape(BLOCK // lo_count, lo_count, up_cols),...  17.5 us
    all_to_all x1, blocking collectives, on_device(): lax.all_to_all(fourth_pass, 'lo', split_axis=0, concat_axis=1, tiled=True)  16.5 us
    all_to_all x1, waiting for transfers between devices, on_device(): lax.all_to_all(first_pass, ('hi', 'mid'), split_axis=1, concat_axis=0, ti...  15.5 us
    all_to_all x1, starting transfers between devices, on_device(): lax.all_to_all(first_pass, ('hi', 'mid'), split_axis=1, concat_axis=0, ti...  7.39 us
    reshape x2, local copies, waits for them, and re-layouts, on_device(): diagonal_factor(up_index, down_index, coupling_seed)  5.05 us
    unnamed x6, local copies, waits for them, and re-layouts  2.63 us
  transfers between devices with their start and end apart: 1, of which 1 were waited for; matrix products, arithmetic and copies ran while one was open for 6% of the time, Pallas kernels for 0%

commit v1 on v0

--- a/solution.py
+++ b/solution.py
@@ -1,13 +1,17 @@
+import functools
+import math
+
 import jax
 import jax.numpy as jnp
 from jax import lax
+from jax.experimental import pallas as pl
+from jax.experimental.pallas import tpu as pltpu
 from jax.sharding import PartitionSpec as P
 
-BLOCK = 512
 SITES = 14
-
-
 COUPLING = 0.06
+AXES = ("hi", "mid", "lo")
+F32, BF16 = jnp.float32, jnp.bfloat16
 
 
 def occupancy(indices):
@@ -25,15 +29,16 @@
     return jnp.exp(-energy)
 
 
-def on_device(amplitudes, hop_blocks, coupling_seed):
+def by_collectives(amplitudes, hop_blocks, coupling_seed):
+    block = hop_blocks.shape[1]
     down_rows, up_cols = amplitudes.shape
     groups = lax.axis_size(("hi", "mid"))
     lo_count = lax.axis_size("lo")
-    split_view = amplitudes.reshape(down_rows, up_cols // BLOCK, BLOCK)
+    split_view = amplitudes.reshape(down_rows, up_cols // block, block)
     first_pass = jnp.einsum(
         "dav,wv->awd", split_view, hop_blocks[0], preferred_element_type=jnp.float32
     ).astype(jnp.bfloat16)
-    local_top = BLOCK // groups
+    local_top = block // groups
     remainder = up_cols // local_top
     first_pass = first_pass.reshape(local_top, remainder, down_rows)
     moved = lax.all_to_all(first_pass, ("hi", "mid"), split_axis=1, concat_axis=0, tiled=True)
@@ -42,13 +47,13 @@
     )
     span_low = remainder // groups
     up_index = (
-        jnp.arange(BLOCK, dtype=jnp.int32)[:, None] * remainder
+        jnp.arange(block, dtype=jnp.int32)[:, None] * remainder
         + lax.axis_index(("hi", "mid")) * span_low
         + jnp.arange(span_low, dtype=jnp.int32)[None, :]
     ).reshape(-1)
     down_index = lax.axis_index("lo") * down_rows + jnp.arange(down_rows, dtype=jnp.int32)
     factor = diagonal_factor(up_index, down_index, coupling_seed).reshape(
-        BLOCK, span_low, down_rows
+        block, span_low, down_rows
     )
     mixed_pass = (second_pass * factor).astype(jnp.bfloat16)
     returned = lax.all_to_all(
@@ -58,7 +63,7 @@
         "ud,ed->eu", returned, hop_blocks[2], preferred_element_type=jnp.float32
     ).astype(jnp.bfloat16)
     gathered = lax.all_to_all(
-        third_pass.reshape(BLOCK // lo_count, lo_count, up_cols),
+        third_pass.reshape(block // lo_count, lo_count, up_cols),
         "lo",
         split_axis=1,
         concat_axis=0,
@@ -73,9 +78,291 @@
     return result
 
 
+def dot_nn(a, b):
+    return lax.dot_general(a, b, (((1,), (0,)), ((), ())), preferred_element_type=F32)
+
+
+def dot_nt(a, b):
+    return lax.dot_general(a, b, (((1,), (1,)), ((), ())), preferred_element_type=F32)
+
+
+def ones_where(shape, condition):
+    rows = lax.broadcasted_iota(jnp.int32, shape, 0)
+    cols = lax.broadcasted_iota(jnp.int32, shape, 1)
+    return jnp.where(condition(rows, cols), 1.0, 0.0).astype(F32).astype(BF16)
+
+
+def step_kernel(
+    counts,
+    low,
+    amp_hbm,
+    hop_hbm,
+    seed_ref,
+    out_ref,
+    amp,
+    hop,
+    packed,
+    moved,
+    factor,
+    mixed,
+    third,
+    fourth,
+    final,
+    in_sem,
+    own_sem,
+    send_sem,
+    recv_sem,
+):
+    n_hi, n_mid, n_lo = counts
+    devices = n_hi * n_mid * n_lo
+    groups = n_hi * n_mid
+    block = hop.shape[1]
+    tops = block // low
+    spans = amp.shape[1] // block
+    my_hi, my_mid, my_lo = (lax.axis_index(name) for name in AXES)
+    me = (my_hi * n_mid + my_mid) * n_lo + my_lo
+    my_group = my_hi * n_mid + my_mid
+
+    amp_in = pltpu.make_async_copy(amp_hbm, amp, in_sem.at[4])
+    amp_in.start()
+    hop_in = [
+        pltpu.make_async_copy(hop_hbm.at[k], hop.at[k], in_sem.at[k]) for k in range(4)
+    ]
+    for copy in hop_in:
+        copy.start()
+
+    def peer(k):
+        rest = k // n_hi
+        hi = lax.rem(my_hi + lax.rem(k, n_hi), n_hi)
+        mid = lax.rem(my_mid + lax.rem(rest, n_mid), n_mid)
+        lo = lax.rem(my_lo + rest // n_mid, n_lo)
+        return hi, mid, lo
+
+    barrier = pltpu.get_barrier_semaphore()
+
+    def greet(k, carry):
+        pl.semaphore_signal(
+            barrier, inc=1, device_id=peer(k), device_id_type=pl.DeviceIdType.MESH
+        )
+        return carry
+
+    lax.fori_loop(1, devices, greet, 0)
+
+    sorter = ones_where((block, block), lambda r, c: c == (r % tops) * low + r // tops)
+    hop_in[0].wait()
+    hop0 = dot_nn(sorter, hop[0]).astype(BF16)
+    amp_in.wait()
+    for b in range(spans):
+        first = dot_nt(hop0, amp[:, b * block : (b + 1) * block]).astype(BF16)
+        packed[:, b] = first.reshape(low, tops, first.shape[1])
+
+    pl.semaphore_wait(barrier, devices - 1)
+
+    def out_copy(hi, mid, lo):
+        target = (hi * n_mid + mid) * n_lo + lo
+        return pltpu.make_async_remote_copy(
+            src_ref=packed.at[target],
+            dst_ref=moved.at[my_lo, my_group],
+            send_sem=send_sem.at[0, target],
+            recv_sem=recv_sem.at[0, me],
+            device_id=(hi, mid, lo),
+            device_id_type=pl.DeviceIdType.MESH,
+        )
+
+    def in_copy(hi, mid, lo):
+        source = (hi * n_mid + mid) * n_lo + lo
+        return pltpu.make_async_remote_copy(
+            src_ref=packed.at[source],
+            dst_ref=moved.at[lo, hi * n_mid + mid],
+            send_sem=send_sem.at[0, source],
+            recv_sem=recv_sem.at[0, source],
+            device_id=(hi, mid, lo),
+            device_id_type=pl.DeviceIdType.MESH,
+        )
+
+    def send_out(k, carry):
+        out_copy(*peer(k)).start()
+        return carry
+
+    lax.fori_loop(1, devices, send_out, 0)
+    own_out = pltpu.make_async_copy(
+        packed.at[me], moved.at[my_lo, my_group], own_sem.at[0]
+    )
+    own_out.start()
+
+    for copy in hop_in[1:]:
+        copy.wait()
+    halves = block // n_lo
+    unzip = ones_where((block, block), lambda r, c: c == (r % halves) * n_lo + r // halves)
+    hop2 = dot_nn(unzip, hop[2]).astype(BF16)
+    rows = lax.broadcasted_iota(jnp.int32, (block, 16), 0) * low + me
+    site_r = lax.broadcasted_iota(jnp.int32, (block, 16), 1)
+    strength = jnp.zeros((block, 16), F32)
+    for i in range(SITES):
+        strength = jnp.where(site_r == i, seed_ref[i].astype(F32), strength)
+    up_part = (((rows >> site_r) & 1).astype(F32) * strength).astype(BF16)
+    cols = lax.broadcasted_iota(jnp.int32, (16, n_lo * block), 1)
+    site_c = lax.broadcasted_iota(jnp.int32, (16, n_lo * block), 0)
+    down_part = ((cols >> site_c) & 1).astype(F32).astype(BF16)
+    for lo in range(n_lo):
+        part = dot_nn(up_part, down_part[:, lo * block : (lo + 1) * block])
+        factor[lo] = jnp.exp(-COUPLING * part)
+
+    own_out.wait()
+
+    def wait_in(k, carry):
+        in_copy(*peer(k)).wait_recv()
+        return carry
+
+    lax.fori_loop(1, devices, wait_in, 0)
+    for lo in range(n_lo):
+        second = dot_nn(hop[1], moved[lo].reshape(block, block))
+        mixed[lo] = (second * factor[lo]).astype(BF16)
+
+    def back_copy(hi, mid, lo):
+        target = (hi * n_mid + mid) * n_lo + lo
+        return pltpu.make_async_remote_copy(
+            src_ref=fourth.at[lo, hi * n_mid + mid],
+            dst_ref=final.at[:, me],
+            send_sem=send_sem.at[1, target],
+            recv_sem=recv_sem.at[1, me],
+            device_id=(hi, mid, lo),
+            device_id_type=pl.DeviceIdType.MESH,
+        )
+
+    def home_copy(hi, mid, lo):
+        source = (hi * n_mid + mid) * n_lo + lo
+        return pltpu.make_async_remote_copy(
+            src_ref=fourth.at[lo, hi * n_mid + mid],
+            dst_ref=final.at[:, source],
+            send_sem=send_sem.at[1, source],
+            recv_sem=recv_sem.at[1, source],
+            device_id=(hi, mid, lo),
+            device_id_type=pl.DeviceIdType.MESH,
+        )
+
+    chunk = block // n_hi
+    for step in [*range(1, n_hi), 0]:
+        hi = lax.rem(my_hi + step, n_hi)
+        at = pl.ds(pl.multiple_of(hi * chunk, chunk), chunk)
+        for lo in range(n_lo):
+            third[lo] = dot_nt(mixed[lo, at, :], hop2).astype(BF16)
+        for r in range(n_lo):
+            total = sum(
+                dot_nt(
+                    third[lo, :, r * halves : (r + 1) * halves],
+                    hop[3, :, lo * halves : (lo + 1) * halves],
+                )
+                for lo in range(n_lo)
+            ).astype(BF16)
+            for lo in range(n_lo):
+                piece = total[:, lo * halves : (lo + 1) * halves]
+                fourth[
+                    lo,
+                    pl.ds(hi * n_mid, n_mid),
+                    :,
+                    :,
+                    r * halves : (r + 1) * halves,
+                ] = piece.reshape(n_mid, spans, tops, halves)
+
+        def send_back(k, carry):
+            mid = lax.rem(my_mid + lax.rem(k, n_mid), n_mid)
+            lo = lax.rem(my_lo + k // n_mid, n_lo)
+            back_copy(hi, mid, lo).start()
+            return carry
+
+        lax.fori_loop(0 if step else 1, n_mid * n_lo, send_back, 0)
+    own_back = pltpu.make_async_copy(
+        fourth.at[my_lo, my_group], final.at[:, me], own_sem.at[1]
+    )
+    own_back.start()
+    zipper = ones_where((block, block), lambda r, c: r == (c % halves) * n_lo + c // halves)
+    own_back.wait()
+
+    def wait_home(k, carry):
+        home_copy(*peer(k)).wait_recv()
+        return carry
+
+    lax.fori_loop(1, devices, wait_home, 0)
+    for b in range(spans):
+        turned = dot_nt(zipper, final[b].reshape(block, block)).astype(BF16)
+        out_ref[:, b * block : (b + 1) * block] = dot_nn(turned, sorter).astype(BF16)
+
+    def drain(k, carry):
+        out_copy(*peer(k)).wait_send()
+        back_copy(*peer(k)).wait_send()
+        return carry
+
+    lax.fori_loop(1, devices, drain, 0)
+
+
+def by_kernel(counts, amplitudes, hop_blocks, coupling_seed):
+    n_hi, n_mid, n_lo = counts
+    groups, devices = n_hi * n_mid, n_hi * n_mid * n_lo
+    block = hop_blocks.shape[1]
+    down_rows, up_cols = amplitudes.shape
+    low = up_cols * groups // block
+    tops = block // low
+    spans = up_cols // block
+    pair = (n_lo, block, block)
+    return pl.pallas_call(
+        functools.partial(step_kernel, counts, low),
+        out_shape=jax.ShapeDtypeStruct((down_rows, up_cols), BF16),
+        in_specs=[
+            pl.BlockSpec(memory_space=pl.ANY),
+            pl.BlockSpec(memory_space=pl.ANY),
+            pl.BlockSpec(memory_space=pltpu.SMEM),
+        ],
+        out_specs=pl.BlockSpec(memory_space=pltpu.VMEM),
+        scratch_shapes=[
+            pltpu.VMEM((down_rows, up_cols), BF16),
+            pltpu.VMEM(hop_blocks.shape, BF16),
+            pltpu.VMEM((low, spans, tops, block), BF16),
+            pltpu.VMEM((n_lo, groups, spans, tops, block), BF16),
+            pltpu.VMEM(pair, F32),
+            pltpu.VMEM(pair, BF16),
+            pltpu.VMEM((n_lo, block // n_hi, block), BF16),
+            pltpu.VMEM((n_lo, groups, spans, tops, block), BF16),
+            pltpu.VMEM((spans, low, tops, block), BF16),
+            pltpu.SemaphoreType.DMA((5,)),
+            pltpu.SemaphoreType.DMA((2,)),
+            pltpu.SemaphoreType.DMA((2, devices)),
+            pltpu.SemaphoreType.DMA((2, devices)),
+        ],
+        compiler_params=pltpu.CompilerParams(
+            collective_id=0, has_side_effects=True, vmem_limit_bytes=48 * 1024 * 1024
+        ),
+        name="trotter_step",
+    )(amplitudes, hop_blocks, coupling_seed)
+
+
+def on_device(counts, amplitudes, hop_blocks, coupling_seed):
+    n_hi, n_mid, n_lo = counts
+    groups, devices = n_hi * n_mid, n_hi * n_mid * n_lo
+    block = hop_blocks.shape[1]
+    down_rows, up_cols = amplitudes.shape
+    low = up_cols * groups // block
+    fits = (
+        low == devices
+        and down_rows == block
+        and up_cols % block == 0
+        and block % (low * 16) == 0
+        and block % (n_lo * 128) == 0
+        and block // groups == (up_cols // block) * (block // low)
+    )
+    if fits:
+        return by_kernel(counts, amplitudes, hop_blocks, coupling_seed)
+    return by_collectives(amplitudes, hop_blocks, coupling_seed)
+
+
 def solution(mesh):
+    counts = tuple(mesh.shape[name] for name in AXES)
     in_specs = (P("lo", ("hi", "mid")), P(), P())
     out_specs = P("lo", ("hi", "mid"))
     return jax.shard_map(
-        on_device, mesh=mesh, in_specs=in_specs, out_specs=out_specs, check_vma=False
-    )
+        functools.partial(on_device, counts),
+        mesh=mesh,
+        in_specs=in_specs,
+        out_specs=out_specs,
+        check_vma=False,
+    )

time: 116 us -> 66 us (0.57)
  the two profiles are of different devices: /device:TPU:0 before, /device:TPU:9 now
where the time goes in v1:
time: 66 us; the launch traced here: 65.9 us
  Pallas kernels  61.4 us (93%)
  local copies, waits for them, and re-layouts  4.44 us (7%)
    pallas_call x1, Pallas kernels, by_kernel(): pl.pallas_call(functools.partial(step_kernel, counts, low), out_shape=jax...  61.4 us
    unnamed x7, local copies, waits for them, and re-layouts  4.44 us

profile of v1, /device:TPU:9, one launch (start us, length us, event | category | flops | bytes accessed | tf_op | source)
XLA Modules:
  0.0 65.9 jit_solution(7413408817973617306)
XLA Ops:
  0.0 0.0 copy-start
  0.0 1.6 %copy-done = bf16[4,512,512]{2,1,0:T(8,128)(2,1)S(1)} copy-done((bf16[4,512,512]{2,1,0:T(8,128)(2,1)S(1)}, bf16[4,512,512]{2,1,0:T(8,128)(2,1)}, u32[]{:S(2)}) %copy-start) | copy-done | bytes 2097176
  1.6 0.0 copy-start.1
  1.6 1.2 %copy-done.1 = bf16[512,1024]{1,0:T(8,128)(2,1)S(1)} copy-done((bf16[512,1024]{1,0:T(8,128)(2,1)S(1)}, bf16[512,1024]{1,0:T(8,128)(2,1)}, u32[]{:S(2)}) %copy-start.1) | copy-done | bytes 1048600
  2.8 0.0 copy-start.2
  2.8 0.7 copy-done.2
  3.5 61.4 %trotter_step.1 = bf16[512,1024]{1,0:T(8,128)(2,1)S(1)} custom-call(bf16[512,1024]{1,0:T(8,128)(2,1)S(1)} %copy-done.1, bf16[4,512,512]{2,1,0:T(8,128)(2,1)S(1)} %copy-done, s32[14]{0:T(128)S(1)} %copy-done.2), custom_call_target="tpu_custom_call" | custom-call | tf_op jit(solution)/shard_map/trotter_step/pallas_call | solution.py:308
  64.9 1.0 %copy.5 = bf16[512,1024]{1,0:T(8,128)(2,1)} copy(bf16[512,1024]{1,0:T(8,128)(2,1)S(1)} %trotter_step.1) | data formatting | bytes 2097152
Async XLA Ops:
  0.0 1.6 %copy-start = (bf16[4,512,512]{2,1,0:T(8,128)(2,1)S(1)}, bf16[4,512,512]{2,1,0:T(8,128)(2,1)}, u32[]{:S(2)}) copy-start(bf16[4,512,512]{2,1,0:T(8,128)(2,1)} %hop_hbm.1) | copy-start | bytes 6291460
  1.6 1.2 %copy-start.1 = (bf16[512,1024]{1,0:T(8,128)(2,1)S(1)}, bf16[512,1024]{1,0:T(8,128)(2,1)}, u32[]{:S(2)}) copy-start(bf16[512,1024]{1,0:T(8,128)(2,1)} %amp_hbm.1) | copy-start | bytes 3145732
  2.8 0.7 copy-start.2

commit v2 on v0

--- a/solution.py
+++ b/solution.py
@@ -1,13 +1,17 @@
+import functools
+
 import jax
 import jax.numpy as jnp
 from jax import lax
+from jax.experimental import pallas as pl
+from jax.experimental.pallas import tpu as pltpu
 from jax.sharding import PartitionSpec as P
 
-BLOCK = 512
 SITES = 14
-
-
 COUPLING = 0.06
+AXES = ("hi", "mid", "lo")
+SIDES = 2
+F32, BF16 = jnp.float32, jnp.bfloat16
 
 
 def occupancy(indices):
@@ -25,15 +29,16 @@
     return jnp.exp(-energy)
 
 
-def on_device(amplitudes, hop_blocks, coupling_seed):
+def by_collectives(amplitudes, hop_blocks, coupling_seed):
+    block = hop_blocks.shape[1]
     down_rows, up_cols = amplitudes.shape
     groups = lax.axis_size(("hi", "mid"))
     lo_count = lax.axis_size("lo")
-    split_view = amplitudes.reshape(down_rows, up_cols // BLOCK, BLOCK)
+    split_view = amplitudes.reshape(down_rows, up_cols // block, block)
     first_pass = jnp.einsum(
         "dav,wv->awd", split_view, hop_blocks[0], preferred_element_type=jnp.float32
     ).astype(jnp.bfloat16)
-    local_top = BLOCK // groups
+    local_top = block // groups
     remainder = up_cols // local_top
     first_pass = first_pass.reshape(local_top, remainder, down_rows)
     moved = lax.all_to_all(first_pass, ("hi", "mid"), split_axis=1, concat_axis=0, tiled=True)
@@ -42,13 +47,13 @@
     )
     span_low = remainder // groups
     up_index = (
-        jnp.arange(BLOCK, dtype=jnp.int32)[:, None] * remainder
+        jnp.arange(block, dtype=jnp.int32)[:, None] * remainder
         + lax.axis_index(("hi", "mid")) * span_low
         + jnp.arange(span_low, dtype=jnp.int32)[None, :]
     ).reshape(-1)
     down_index = lax.axis_index("lo") * down_rows + jnp.arange(down_rows, dtype=jnp.int32)
     factor = diagonal_factor(up_index, down_index, coupling_seed).reshape(
-        BLOCK, span_low, down_rows
+        block, span_low, down_rows
     )
     mixed_pass = (second_pass * factor).astype(jnp.bfloat16)
     returned = lax.all_to_all(
@@ -58,7 +63,7 @@
         "ud,ed->eu", returned, hop_blocks[2], preferred_element_type=jnp.float32
     ).astype(jnp.bfloat16)
     gathered = lax.all_to_all(
-        third_pass.reshape(BLOCK // lo_count, lo_count, up_cols),
+        third_pass.reshape(block // lo_count, lo_count, up_cols),
         "lo",
         split_axis=1,
         concat_axis=0,
@@ -73,9 +78,326 @@
     return result
 
 
+def dot_nn(a, b):
+    return lax.dot_general(a, b, (((1,), (0,)), ((), ())), preferred_element_type=F32)
+
+
+def dot_nt(a, b):
+    return lax.dot_general(a, b, (((1,), (1,)), ((), ())), preferred_element_type=F32)
+
+
+def ones_where(shape, condition):
+    rows = lax.broadcasted_iota(jnp.int32, shape, 0)
+    cols = lax.broadcasted_iota(jnp.int32, shape, 1)
+    return jnp.where(condition(rows, cols), 1.0, 0.0).astype(F32).astype(BF16)
+
+
+def step_kernel(
+    counts,
+    low,
+    amp_hbm,
+    hop_hbm,
+    seed_ref,
+    out_ref,
+    amp,
+    hop,
+    hop0,
+    hop1,
+    hop2,
+    hop3,
+    packed,
+    moved,
+    factor,
+    third,
+    fourth,
+    final,
+    in_sem,
+    own_sem,
+    send_sem,
+    recv_sem,
+):
+    n_hi, n_mid, n_lo = counts
+    devices = n_hi * n_mid * n_lo
+    groups = n_hi * n_mid
+    near = groups // SIDES
+    block = hop.shape[1]
+    tops = block // low
+    spans = amp.shape[0]
+    halves = block // n_lo
+    rows = near * tops
+    my_hi, my_mid, my_lo = (lax.axis_index(name) for name in AXES)
+    my_group = my_hi * n_mid + my_mid
+    my_side = my_group // near
+    me = my_group * n_lo + my_lo
+    mesh_id = pl.DeviceIdType.MESH
+
+    hop_in = [
+        pltpu.make_async_copy(hop_hbm.at[k], hop.at[k], in_sem.at[k]) for k in range(4)
+    ]
+    amp_in = [
+        pltpu.make_async_copy(
+            amp_hbm.at[:, b * block : (b + 1) * block], amp.at[b], in_sem.at[4 + b]
+        )
+        for b in range(spans)
+    ]
+    hop_in[0].start()
+    for copy in amp_in:
+        copy.start()
+    for copy in hop_in[1:]:
+        copy.start()
+
+    def spot(side_step, lo_step, k):
+        side = lax.rem(my_side + side_step, SIDES)
+        group = side * near + lax.rem(lax.rem(my_group, near) + k, near)
+        return group, lax.rem(my_lo + lo_step, n_lo)
+
+    def where(group, lo):
+        return group // n_mid, lax.rem(group, n_mid), lo
+
+    def each(side_step, lo_step, act):
+        def body(k, carry):
+            act(*spot(side_step, lo_step, k))
+            return carry
+
+        lax.fori_loop(1 if side_step == lo_step == 0 else 0, near, body, 0)
+
+    side_steps = [*range(1, SIDES), 0]
+    barrier = pltpu.get_barrier_semaphore()
+
+    def greet(group, lo):
+        pl.semaphore_signal(
+            barrier, inc=1, device_id=where(group, lo), device_id_type=mesh_id
+        )
+
+    for lo_step in range(n_lo):
+        for side_step in side_steps:
+            each(side_step, lo_step, greet)
+
+    def out_copy(group, lo):
+        return pltpu.make_async_remote_copy(
+            src_ref=packed.at[lo, group],
+            dst_ref=moved.at[my_lo, my_group],
+            send_sem=send_sem.at[0, group * n_lo + lo],
+            recv_sem=recv_sem.at[0, me],
+            device_id=where(group, lo),
+            device_id_type=mesh_id,
+        )
+
+    def in_copy(group, lo):
+        return pltpu.make_async_remote_copy(
+            src_ref=packed.at[lo, group],
+            dst_ref=moved.at[lo, group],
+            send_sem=send_sem.at[0, group * n_lo + lo],
+            recv_sem=recv_sem.at[0, group * n_lo + lo],
+            device_id=where(group, lo),
+            device_id_type=mesh_id,
+        )
+
+    def back_copy(b, group, lo):
+        return pltpu.make_async_remote_copy(
+            src_ref=fourth.at[lo, b, group],
+            dst_ref=final.at[b, my_lo * groups + my_group],
+            send_sem=send_sem.at[1 + b, group * n_lo + lo],
+            recv_sem=recv_sem.at[1 + b, me],
+            device_id=where(group, lo),
+            device_id_type=mesh_id,
+        )
+
+    def home_copy(b, group, lo):
+        return pltpu.make_async_remote_copy(
+            src_ref=fourth.at[lo, b, group],
+            dst_ref=final.at[b, lo * groups + group],
+            send_sem=send_sem.at[1 + b, group * n_lo + lo],
+            recv_sem=recv_sem.at[1 + b, group * n_lo + lo],
+            device_id=where(group, lo),
+            device_id_type=mesh_id,
+        )
+
+    sorter = ones_where(
+        (block, block),
+        lambda r, c: c == (r % tops) * low + (r // tops % groups) * n_lo + r // (tops * groups),
+    )
+    hop_in[0].wait()
+    hop0[...] = dot_nn(sorter, hop[0]).astype(BF16).reshape(hop0.shape)
+    for copy in amp_in:
+        copy.wait()
+    greeted = False
+    for lo_step in range(n_lo):
+        lo = lax.rem(my_lo + lo_step, n_lo)
+        for side_step in side_steps:
+            side = lax.rem(my_side + side_step, SIDES)
+            for b in range(spans):
+                first = dot_nt(hop0[lo, side], amp[b]).astype(BF16)
+                packed[lo, pl.ds(side * near, near), b] = first.reshape(near, tops, block)
+            if not greeted:
+                pl.semaphore_wait(barrier, devices - 1)
+                greeted = True
+            each(side_step, lo_step, lambda g, l: out_copy(g, l).start())
+    own_out = pltpu.make_async_copy(
+        packed.at[my_lo, my_group], moved.at[my_lo, my_group], own_sem.at[0]
+    )
+    own_out.start()
+
+    for copy in hop_in[1:]:
+        copy.wait()
+    for b in range(spans):
+        hop1[b] = (
+            hop[1].reshape(groups, spans, tops, block)[:, b].reshape(SIDES, rows, block)
+        )
+    unzip = ones_where((block, block), lambda r, c: c == (r % halves) * n_lo + r // halves)
+    hop2[...] = dot_nn(unzip, hop[2]).T.astype(BF16)
+    hop3[...] = hop[3].astype(F32).T.astype(BF16).reshape(hop3.shape)
+    at = lax.broadcasted_iota(jnp.int32, (block, 16), 0)
+    span, group, top = at // (tops * groups), at // tops % groups, at % tops
+    ups = ((group * spans + span) * tops + top) * low + me
+    site_r = lax.broadcasted_iota(jnp.int32, (block, 16), 1)
+    strength = jnp.zeros((block, 16), F32)
+    for i in range(SITES):
+        strength = jnp.where(site_r == i, seed_ref[i].astype(F32), strength)
+    up_part = (((ups >> site_r) & 1).astype(F32) * strength).astype(BF16)
+    downs = lax.broadcasted_iota(jnp.int32, (16, n_lo * block), 1)
+    site_c = lax.broadcasted_iota(jnp.int32, (16, n_lo * block), 0)
+    down_part = ((downs >> site_c) & 1).astype(F32).astype(BF16)
+    for lo in range(n_lo):
+        part = dot_nn(up_part, down_part[:, lo * block : (lo + 1) * block])
+        factor[lo] = jnp.exp(-COUPLING * part).reshape(factor.shape[1:])
+    own_out.wait()
+
+    def two_passes(lo, b, side):
+        second = dot_nn(hop1[b, side], moved[lo].reshape(block, block))
+        mixed = (second * factor[lo, b, side]).astype(BF16)
+        return dot_nn(mixed, hop2[...]).astype(BF16)
+
+    for lo_step in range(n_lo):
+        for side_step in side_steps:
+            each(side_step, lo_step, lambda g, l: in_copy(g, l).wait_recv())
+        lo = lax.rem(my_lo + lo_step, n_lo)
+        if lo_step < n_lo - 1:
+            for b in range(spans):
+                for side in range(SIDES):
+                    third[lo_step, b, side] = two_passes(lo, b, side)
+    last_lo = lo
+    for b in range(spans):
+        for side_step in side_steps:
+            side = lax.rem(my_side + side_step, SIDES)
+            thirds = [third[k, b, side] for k in range(n_lo - 1)]
+            thirds.append(two_passes(last_lo, b, side))
+            for r in range(n_lo):
+                total = sum(
+                    dot_nn(
+                        thirds[k][:, r * halves : (r + 1) * halves],
+                        hop3[lax.rem(my_lo + k, n_lo)],
+                    )
+                    for k in range(n_lo)
+                ).astype(BF16)
+                for lo in range(n_lo):
+                    piece = total[:, lo * halves : (lo + 1) * halves]
+                    fourth[
+                        lo, b, pl.ds(side * near, near), :, r * halves : (r + 1) * halves
+                    ] = piece.reshape(near, tops, halves)
+            for lo_step in range(n_lo):
+                each(side_step, lo_step, lambda g, l: back_copy(b, g, l).start())
+    own_back = [
+        pltpu.make_async_copy(
+            fourth.at[my_lo, b, my_group],
+            final.at[b, my_lo * groups + my_group],
+            own_sem.at[1 + b],
+        )
+        for b in range(spans)
+    ]
+    for copy in own_back:
+        copy.start()
+    zipper = ones_where((block, block), lambda r, c: r == (c % halves) * n_lo + c // halves)
+    for b in range(spans):
+        own_back[b].wait()
+        for lo_step in range(n_lo):
+            for side_step in side_steps:
+                each(side_step, lo_step, lambda g, l: home_copy(b, g, l).wait_recv())
+        turned = dot_nt(zipper, final[b].reshape(block, block)).astype(BF16)
+        out_ref[:, b * block : (b + 1) * block] = dot_nn(turned, sorter).astype(BF16)
+
+    def drain(group, lo):
+        out_copy(group, lo).wait_send()
+        for b in range(spans):
+            back_copy(b, group, lo).wait_send()
+
+    for lo_step in range(n_lo):
+        for side_step in side_steps:
+            each(side_step, lo_step, drain)
+
+
+def by_kernel(counts, amplitudes, hop_blocks, coupling_seed):
+    n_hi, n_mid, n_lo = counts
+    groups, devices = n_hi * n_mid, n_hi * n_mid * n_lo
+    block = hop_blocks.shape[1]
+    down_rows, up_cols = amplitudes.shape
+    low = up_cols * groups // block
+    tops = block // low
+    spans = up_cols // block
+    rows = groups // SIDES * tops
+    return pl.pallas_call(
+        functools.partial(step_kernel, counts, low),
+        out_shape=jax.ShapeDtypeStruct((down_rows, up_cols), BF16),
+        in_specs=[
+            pl.BlockSpec(memory_space=pltpu.HBM),
+            pl.BlockSpec(memory_space=pltpu.HBM),
+            pl.BlockSpec(memory_space=pltpu.SMEM),
+        ],
+        out_specs=pl.BlockSpec(memory_space=pltpu.VMEM),
+        scratch_shapes=[
+            pltpu.VMEM((spans, block, block), BF16),
+            pltpu.VMEM(hop_blocks.shape, BF16),
+            pltpu.VMEM((n_lo, SIDES, rows, block), BF16),
+            pltpu.VMEM((spans, SIDES, rows, block), BF16),
+            pltpu.VMEM((block, block), BF16),
+            pltpu.VMEM((n_lo, block // n_lo, block), BF16),
+            pltpu.VMEM((n_lo, groups, spans, tops, block), BF16),
+            pltpu.VMEM((n_lo, groups, spans, tops, block), BF16),
+            pltpu.VMEM((n_lo, spans, SIDES, rows, block), F32),
+            pltpu.VMEM((n_lo - 1, spans, SIDES, rows, block), BF16),
+            pltpu.VMEM((n_lo, spans, groups, tops, block), BF16),
+            pltpu.VMEM((spans, low, tops, block), BF16),
+            pltpu.SemaphoreType.DMA((4 + spans,)),
+            pltpu.SemaphoreType.DMA((1 + spans,)),
+            pltpu.SemaphoreType.DMA((1 + spans, devices)),
+            pltpu.SemaphoreType.DMA((1 + spans, devices)),
+        ],
+        compiler_params=pltpu.CompilerParams(
+            collective_id=0, has_side_effects=True, vmem_limit_bytes=60 * 1024 * 1024
+        ),
+        name="trotter_step",
+    )(amplitudes, hop_blocks, coupling_seed)
+
+
+def on_device(counts, amplitudes, hop_blocks, coupling_seed):
+    n_hi, n_mid, n_lo = counts
+    groups, devices = n_hi * n_mid, n_hi * n_mid * n_lo
+    block = hop_blocks.shape[1]
+    down_rows, up_cols = amplitudes.shape
+    low = up_cols * groups // block
+    fits = (
+        low == devices
+        and down_rows == block
+        and up_cols % block == 0
+        and block % (low * 16) == 0
+        and n_lo > 1
+        and n_hi % SIDES == 0
+        and block % (n_lo * 128) == 0
+        and block // groups == (up_cols // block) * (block // low)
+    )
+    if fits:
+        return by_kernel(counts, amplitudes, hop_blocks, coupling_seed)
+    return by_collectives(amplitudes, hop_blocks, coupling_seed)
+
+
 def solution(mesh):
+    counts = tuple(mesh.shape[name] for name in AXES)
     in_specs = (P("lo", ("hi", "mid")), P(), P())
     out_specs = P("lo", ("hi", "mid"))
     return jax.shard_map(
-        on_device, mesh=mesh, in_specs=in_specs, out_specs=out_specs, check_vma=False
-    )
+        functools.partial(on_device, counts),
+        mesh=mesh,
+        in_specs=in_specs,
+        out_specs=out_specs,
+        check_vma=False,
+    )

time: 116 us -> 64.1 us (0.55)
  blocking collectives: 65.2 us -> 0 us
  Pallas kernels: 0 us -> 61.7 us
  waiting for transfers between devices: 15.5 us -> 0 us
  local copies, waits for them, and re-layouts: 15.7 us -> 2.26 us
  matrix products: 9.51 us -> 0 us
  starting transfers between devices: 7.39 us -> 0 us
  other arithmetic: 1.59 us -> 0 us
    all_to_all x3 -> x0, blocking collectives: 65.2 us -> none  [the longest x1 31.3 us: on_device(): lax.all_to_all(mixed_pass, ('hi', 'mid'), split_axis=0, concat_axis=1, ti...]
    pallas_call x0 -> x1, Pallas kernels: none -> 61.7 us  [by_kernel(): pl.pallas_call(functools.partial(step_kernel, counts, low), out_shape=jax...]
    all_to_all x1 -> x0, waiting for transfers between devices: 15.5 us -> none  [on_device(): lax.all_to_all(first_pass, ('hi', 'mid'), split_axis=1, concat_axis=0, ti...]
    dot_general x5 -> x0, matrix products: 9.51 us -> none  [the longest x1 2.13 us: on_device(): jnp.einsum('dav,wv->awd', split_view, hop_blocks[0], preferred_element_ty...]
    reshape x7 -> x0, local copies, waits for them, and re-layouts: 8.97 us -> none  [the longest x2 5.05 us: on_device(): diagonal_factor(up_index, down_index, coupling_seed)]
    all_to_all x1 -> x0, starting transfers between devices: 7.39 us -> none  [on_device(): lax.all_to_all(first_pass, ('hi', 'mid'), split_axis=1, concat_axis=0, ti...]
    all_to_all x4 -> x0, local copies, waits for them, and re-layouts: 2.39 us -> none  [the longest x2 1.25 us: on_device(): lax.all_to_all(mixed_pass, ('hi', 'mid'), split_axis=0, concat_axis=1, ti...]
    convert_element_type x2 -> x0, local copies, waits for them, and re-layouts: 1.5 us -> none  [the longest x1 0.98 us: on_device(): mixed_pass = (second_pass * factor).astype(jnp.bfloat16)]
  transfers between devices with their start and end apart: 1 -> 0, of which waited for: 1 -> 0; matrix products, arithmetic and copies ran while one was open for 6% -> 0% of each run, Pallas kernels for 0% -> 0%
where the time goes in v2:
time: 64.1 us; the launch traced here: 63.9 us
  Pallas kernels  61.7 us (96%)
  local copies, waits for them, and re-layouts  2.26 us (4%)
    pallas_call x1, Pallas kernels, by_kernel(): pl.pallas_call(functools.partial(step_kernel, counts, low), out_shape=jax...  61.7 us
    unnamed x1, local copies, waits for them, and re-layouts  2.26 us

profile of v2, /device:TPU:0, one launch (start us, length us, event | category | flops | bytes accessed | tf_op | source)
XLA Modules:
  0.0 63.9 jit_solution(5191214597104680970)
XLA Ops:
  0.0 61.7 %trotter_step.1 = bf16[512,1024]{1,0:T(8,128)(2,1)} custom-call(bf16[512,1024]{1,0:T(8,128)(2,1)} %amp_hbm.1, bf16[4,512,512]{2,1,0:T(8,128)(2,1)} %hop_hbm.1, s32[14]{0:T(128)} %seed_ref.1), custom_call_target="tpu_custom_call" | custom-call | tf_op jit(solution)/shard_map/trotter_step/pallas_call | solution.py:338
  61.7 2.3 %copy.5 = bf16[512,1024]{1,0:T(8,128)(2,1)} copy(bf16[512,1024]{1,0:T(8,128)(2,1)} %trotter_step.1) | data formatting | bytes 2097152

commit v3 on v2

--- a/solution.py
+++ b/solution.py
@@ -222,10 +222,10 @@
     for copy in amp_in:
         copy.wait()
     greeted = False
-    for lo_step in range(n_lo):
-        lo = lax.rem(my_lo + lo_step, n_lo)
-        for side_step in side_steps:
-            side = lax.rem(my_side + side_step, SIDES)
+    for side_step in side_steps:
+        side = lax.rem(my_side + side_step, SIDES)
+        for lo_step in range(n_lo):
+            lo = lax.rem(my_lo + lo_step, n_lo)
             for b in range(spans):
                 first = dot_nt(hop0[lo, side], amp[b]).astype(BF16)
                 packed[lo, pl.ds(side * near, near), b] = first.reshape(near, tops, block)
@@ -277,8 +277,8 @@
                 for side in range(SIDES):
                     third[lo_step, b, side] = two_passes(lo, b, side)
     last_lo = lo
-    for b in range(spans):
-        for side_step in side_steps:
+    for side_step in side_steps:
+        for b in range(spans):
             side = lax.rem(my_side + side_step, SIDES)
             thirds = [third[k, b, side] for k in range(n_lo - 1)]
             thirds.append(two_passes(last_lo, b, side))

time: 64.1 us -> 64.2 us (level)
  no operation moved by 1% of the time
where the time goes in v3:
time: 64.2 us; the launch traced here: 64.1 us
  Pallas kernels  61.8 us (96%)
  local copies, waits for them, and re-layouts  2.26 us (4%)
    pallas_call x1, Pallas kernels, by_kernel(): pl.pallas_call(functools.partial(step_kernel, counts, low), out_shape=jax...  61.8 us
    unnamed x1, local copies, waits for them, and re-layouts  2.26 us

profile of v3, /device:TPU:0, one launch (start us, length us, event | category | flops | bytes accessed | tf_op | source)
XLA Modules:
  0.0 64.1 jit_solution(15700594954910345712)
XLA Ops:
  0.0 61.8 %trotter_step.1 = bf16[512,1024]{1,0:T(8,128)(2,1)} custom-call(bf16[512,1024]{1,0:T(8,128)(2,1)} %amp_hbm.1, bf16[4,512,512]{2,1,0:T(8,128)(2,1)} %hop_hbm.1, s32[14]{0:T(128)} %seed_ref.1), custom_call_target="tpu_custom_call" | custom-call | tf_op jit(solution)/shard_map/trotter_step/pallas_call | solution.py:338
  61.8 2.3 %copy.5 = bf16[512,1024]{1,0:T(8,128)(2,1)} copy(bf16[512,1024]{1,0:T(8,128)(2,1)} %trotter_step.1) | data formatting | bytes 2097152

commit v4 on v3

--- a/solution.py
+++ b/solution.py
@@ -101,7 +101,6 @@
     out_ref,
     amp,
     hop,
-    hop0,
     hop1,
     hop2,
     hop3,
@@ -143,8 +142,6 @@
     hop_in[0].start()
     for copy in amp_in:
         copy.start()
-    for copy in hop_in[1:]:
-        copy.start()
 
     def spot(side_step, lo_step, k):
         side = lax.rem(my_side + side_step, SIDES)
@@ -213,25 +210,27 @@
             device_id_type=mesh_id,
         )
 
-    sorter = ones_where(
-        (block, block),
-        lambda r, c: c == (r % tops) * low + (r // tops % groups) * n_lo + r // (tops * groups),
-    )
     hop_in[0].wait()
-    hop0[...] = dot_nn(sorter, hop[0]).astype(BF16).reshape(hop0.shape)
-    for copy in amp_in:
-        copy.wait()
     greeted = False
     for side_step in side_steps:
         side = lax.rem(my_side + side_step, SIDES)
         for lo_step in range(n_lo):
             lo = lax.rem(my_lo + lo_step, n_lo)
+            picker = ones_where(
+                (rows, block),
+                lambda r, c: c == (r % tops) * low + (side * near + r // tops) * n_lo + lo,
+            )
+            weights = dot_nn(picker, hop[0]).astype(BF16)
             for b in range(spans):
-                first = dot_nt(hop0[lo, side], amp[b]).astype(BF16)
+                if not greeted:
+                    amp_in[b].wait()
+                first = dot_nt(weights, amp[b]).astype(BF16)
                 packed[lo, pl.ds(side * near, near), b] = first.reshape(near, tops, block)
             if not greeted:
                 pl.semaphore_wait(barrier, devices - 1)
                 greeted = True
+                for copy in hop_in[1:]:
+                    copy.start()
             each(side_step, lo_step, lambda g, l: out_copy(g, l).start())
     own_out = pltpu.make_async_copy(
         packed.at[my_lo, my_group], moved.at[my_lo, my_group], own_sem.at[0]
@@ -307,6 +306,10 @@
     ]
     for copy in own_back:
         copy.start()
+    sorter = ones_where(
+        (block, block),
+        lambda r, c: c == (r % tops) * low + (r // tops % groups) * n_lo + r // (tops * groups),
+    )
     zipper = ones_where((block, block), lambda r, c: r == (c % halves) * n_lo + c // halves)
     for b in range(spans):
         own_back[b].wait()
@@ -347,7 +350,6 @@
         scratch_shapes=[
             pltpu.VMEM((spans, block, block), BF16),
             pltpu.VMEM(hop_blocks.shape, BF16),
-            pltpu.VMEM((n_lo, SIDES, rows, block), BF16),
             pltpu.VMEM((spans, SIDES, rows, block), BF16),
             pltpu.VMEM((block, block), BF16),
             pltpu.VMEM((n_lo, block // n_lo, block), BF16),

time: 64.2 us -> 64.3 us (level)
  no operation moved by 1% of the time
where the time goes in v4:
time: 64.3 us; the launch traced here: 64.1 us
  Pallas kernels  61.8 us (96%)
  local copies, waits for them, and re-layouts  2.26 us (4%)
    pallas_call x1, Pallas kernels, by_kernel(): pl.pallas_call(functools.partial(step_kernel, counts, low), out_shape=jax...  61.8 us
    unnamed x1, local copies, waits for them, and re-layouts  2.26 us

profile of v4, /device:TPU:0, one launch (start us, length us, event | category | flops | bytes accessed | tf_op | source)
XLA Modules:
  0.0 64.1 jit_solution(12327456248616700527)
XLA Ops:
  0.0 61.8 %trotter_step.1 = bf16[512,1024]{1,0:T(8,128)(2,1)} custom-call(bf16[512,1024]{1,0:T(8,128)(2,1)} %amp_hbm.1, bf16[4,512,512]{2,1,0:T(8,128)(2,1)} %hop_hbm.1, s32[14]{0:T(128)} %seed_ref.1), custom_call_target="tpu_custom_call" | custom-call | tf_op jit(solution)/shard_map/trotter_step/pallas_call | solution.py:341
  61.8 2.3 %copy.5 = bf16[512,1024]{1,0:T(8,128)(2,1)} copy(bf16[512,1024]{1,0:T(8,128)(2,1)} %trotter_step.1) | data formatting | bytes 2097152

commit v5 on v3

--- a/solution.py
+++ b/solution.py
@@ -147,19 +147,20 @@
         copy.start()
 
     def spot(side_step, lo_step, k):
-        side = lax.rem(my_side + side_step, SIDES)
-        group = side * near + lax.rem(lax.rem(my_group, near) + k, near)
+        group = lax.bitwise_xor(my_group, side_step * near + k)
         return group, lax.rem(my_lo + lo_step, n_lo)
 
     def where(group, lo):
         return group // n_mid, lax.rem(group, n_mid), lo
 
-    def each(side_step, lo_step, act):
+    def each(side_step, lo_step, act, begin=0, end=near):
         def body(k, carry):
             act(*spot(side_step, lo_step, k))
             return carry
 
-        lax.fori_loop(1 if side_step == lo_step == 0 else 0, near, body, 0)
+        if side_step == lo_step == 0:
+            begin = max(begin, 1)
+        lax.fori_loop(begin, end, body, 0)
 
     side_steps = [*range(1, SIDES), 0]
     barrier = pltpu.get_barrier_semaphore()
@@ -232,7 +233,9 @@
             if not greeted:
                 pl.semaphore_wait(barrier, devices - 1)
                 greeted = True
-            each(side_step, lo_step, lambda g, l: out_copy(g, l).start())
+            each(side_step, lo_step, lambda g, l: out_copy(g, l).start(), end=near // 2)
+        for lo_step in range(n_lo):
+            each(side_step, lo_step, lambda g, l: out_copy(g, l).start(), near // 2)
     own_out = pltpu.make_async_copy(
         packed.at[my_lo, my_group], moved.at[my_lo, my_group], own_sem.at[0]
     )
@@ -295,8 +298,15 @@
                     fourth[
                         lo, b, pl.ds(side * near, near), :, r * halves : (r + 1) * halves
                     ] = piece.reshape(near, tops, halves)
-            for lo_step in range(n_lo):
-                each(side_step, lo_step, lambda g, l: back_copy(b, g, l).start())
+            for begin in (0, near // 2):
+                for lo_step in range(n_lo):
+                    each(
+                        side_step,
+                        lo_step,
+                        lambda g, l: back_copy(b, g, l).start(),
+                        begin,
+                        begin + near // 2,
+                    )
     own_back = [
         pltpu.make_async_copy(
             fourth.at[my_lo, b, my_group],
@@ -382,6 +392,8 @@
         and block % (low * 16) == 0
         and n_lo > 1
         and n_hi % SIDES == 0
+        and groups & (groups - 1) == 0
+        and groups >= 2 * SIDES
         and block % (n_lo * 128) == 0
         and block // groups == (up_cols // block) * (block // low)
     )

time: 64.2 us -> 66.5 us (1.036)
  Pallas kernels: 61.8 us -> 64.1 us
    pallas_call x1, Pallas kernels: 61.8 us -> 64.1 us  [by_kernel(): pl.pallas_call(functools.partial(step_kernel, counts, low), out_shape=jax...]
where the time goes in v5:
time: 66.5 us; the launch traced here: 66.4 us
  Pallas kernels  64.1 us (96%)
  local copies, waits for them, and re-layouts  2.26 us (3%)
    pallas_call x1, Pallas kernels, by_kernel(): pl.pallas_call(functools.partial(step_kernel, counts, low), out_shape=jax...  64.1 us
    unnamed x1, local copies, waits for them, and re-layouts  2.26 us

profile of v5, /device:TPU:0, one launch (start us, length us, event | category | flops | bytes accessed | tf_op | source)
XLA Modules:
  0.0 66.4 jit_solution(8603032222818163811)
XLA Ops:
  0.0 64.1 %trotter_step.1 = bf16[512,1024]{1,0:T(8,128)(2,1)} custom-call(bf16[512,1024]{1,0:T(8,128)(2,1)} %amp_hbm.1, bf16[4,512,512]{2,1,0:T(8,128)(2,1)} %hop_hbm.1, s32[14]{0:T(128)} %seed_ref.1), custom_call_target="tpu_custom_call" | custom-call | tf_op jit(solution)/shard_map/trotter_step/pallas_call | solution.py:348
  64.1 2.3 %copy.5 = bf16[512,1024]{1,0:T(8,128)(2,1)} copy(bf16[512,1024]{1,0:T(8,128)(2,1)} %trotter_step.1) | data formatting | bytes 2097152

commit v6 on v2

--- a/solution.py
+++ b/solution.py
@@ -148,7 +148,7 @@
 
     def spot(side_step, lo_step, k):
         side = lax.rem(my_side + side_step, SIDES)
-        group = side * near + lax.rem(lax.rem(my_group, near) + k, near)
+        group = side * near + lax.rem(lax.rem(my_group, near) + 3 * k, near)
         return group, lax.rem(my_lo + lo_step, n_lo)
 
     def where(group, lo):
@@ -382,6 +382,7 @@
         and block % (low * 16) == 0
         and n_lo > 1
         and n_hi % SIDES == 0
+        and groups // SIDES % 3 != 0
         and block % (n_lo * 128) == 0
         and block // groups == (up_cols // block) * (block // low)
     )

time: 64.1 us -> 64.7 us (level)
  no operation moved by 1% of the time
where the time goes in v6:
time: 64.7 us; the launch traced here: 64.6 us
  Pallas kernels  62.3 us (96%)
  local copies, waits for them, and re-layouts  2.26 us (3%)
    pallas_call x1, Pallas kernels, by_kernel(): pl.pallas_call(functools.partial(step_kernel, counts, low), out_shape=jax...  62.3 us
    unnamed x1, local copies, waits for them, and re-layouts  2.26 us

profile of v6, /device:TPU:0, one launch (start us, length us, event | category | flops | bytes accessed | tf_op | source)
XLA Modules:
  0.0 64.6 jit_solution(9055655933232128019)
XLA Ops:
  0.0 62.3 %trotter_step.1 = bf16[512,1024]{1,0:T(8,128)(2,1)} custom-call(bf16[512,1024]{1,0:T(8,128)(2,1)} %amp_hbm.1, bf16[4,512,512]{2,1,0:T(8,128)(2,1)} %hop_hbm.1, s32[14]{0:T(128)} %seed_ref.1), custom_call_target="tpu_custom_call" | custom-call | tf_op jit(solution)/shard_map/trotter_step/pallas_call | solution.py:338
  62.3 2.3 %copy.5 = bf16[512,1024]{1,0:T(8,128)(2,1)} copy(bf16[512,1024]{1,0:T(8,128)(2,1)} %trotter_step.1) | data formatting | bytes 2097152
